TPU v7x, 128 devices: a whole 4x4x4 slice. The times are simulated.
128 devices in a mesh: prow: 32 (over x, z_lo, y), pcol: 4 (over z_hi, core).
Axes of the slice: x: 4, y: 4, z: 4 (z_hi: 2, z_lo: 2; z = z_hi * 2 + z_lo), core: 2. Of those that a mesh axis runs over, the one named last changes fastest.
Arguments:
- inverse_band: float32 [4096, 4096], P('prow', 'pcol'), may hold values from -0.09375 to 0.09375
- factor_panel: float32 [2, 4096, 512], P(None, 'prow', 'pcol'), may hold values from -0.6 to 0.6
- diag_inverse: float32 [2, 512, 512], replicated, may hold values from -1 to 2, as said below
- ancestors: int32 [2, 63], replicated, may hold values from 0 to 63, as said below
- counts: int32 [2], replicated, may hold values from 1 to 63, as said below
Outputs:
- new_column: float32 [2, 4096, 512], P(None, 'prow', 'pcol')
- diag_block: float32 [2, 512, 512], P(None, 'prow', 'pcol')
Inputs may be any that keep to these rules, and one draw needn't show every extreme that they name: Each row holds distinct block numbers; its first counts[s] entries are in increasing order and include 63; the entries after them are other block numbers, which are not ancestors. One of the two counts is 63; the other is below 63. `diag_inverse`: lower triangular; diagonal entries from 0.5 to 2.
All inputs are finite; a program needn't handle non-finite values.
Results may differ from a plain program's by a relative error of at most 0.000073.
Values sent between devices are 32-bit elements; how exact they have to be, the bound alone decides.
No kernel may reach another device: no remote copies, remote signals or barrier semaphores. Data moves between devices by JAX's collectives and lax.ppermute only.
A program may use at most 64 MiB of HBM per device.

v0:
```python
import jax
import jax.numpy as jnp
from jax import lax
from jax.sharding import PartitionSpec as P

W = 512
BS = 64
precise = lax.Precision.HIGHEST


def local(inverse_band, factor_panel, diag_inverse, ancestors, counts):
    row_index = lax.axis_index("prow")
    col_index = lax.axis_index("pcol")
    row_devices = lax.axis_size("prow")
    col_devices = lax.axis_size("pcol")
    supernodes = factor_panel.shape[0]
    band_rows = factor_panel.shape[1]
    blocks = band_rows // BS
    quarter = W // col_devices
    block_ids = jnp.arange(blocks, dtype=jnp.int32) * row_devices + row_index
    filled = jnp.arange(ancestors.shape[1], dtype=jnp.int32)[None, :] < counts[:, None]
    matches = (ancestors[:, :, None] == block_ids[None, None, :]) & filled[:, :, None]
    members = jnp.any(matches, axis=1).astype(jnp.float32)
    row_mask = jnp.repeat(members, BS, axis=1)[:, :, None]
    full_panel = lax.all_gather(factor_panel, "pcol", axis=2, tiled=True)
    scaled_panel = (
        jnp.einsum("srk,skw->srw", full_panel, diag_inverse, precision=precise) * row_mask
    )
    own_part = lax.dynamic_slice_in_dim(scaled_panel, col_index * quarter, quarter, 2)
    collected = lax.all_gather(own_part, "prow", axis=1, tiled=True)
    grouped = collected.reshape(
        supernodes, row_devices // col_devices, col_devices, band_rows, quarter
    )
    incoming = lax.all_to_all(grouped, "pcol", split_axis=2, concat_axis=4, tiled=True)
    stacked = incoming.reshape(incoming.shape[0], -1, incoming.shape[-1])
    partial_sums = jnp.einsum("rc,scw->srw", inverse_band, stacked, precision=precise)
    summed = lax.psum_scatter(partial_sums, "pcol", scatter_dimension=2, tiled=True)
    applied = summed * row_mask
    new_column = -applied
    diag_rows = W // row_devices
    product = jnp.einsum("src,srw->csw", scaled_panel, applied, precision=precise)
    reduced = lax.psum_scatter(
        product.reshape(lax.axis_size("prow") * diag_rows, -1),
        "prow",
        scatter_dimension=0,
        tiled=True,
    )
    reduced = reduced.reshape(diag_rows, supernodes, quarter).transpose(1, 0, 2)
    row_factor = lax.dynamic_slice_in_dim(diag_inverse, row_index * diag_rows, diag_rows, 2)
    col_factor = lax.dynamic_slice_in_dim(diag_inverse, col_index * quarter, quarter, 2)
    diag_block = jnp.einsum("skr,skw->srw", row_factor, col_factor, precision=precise) + reduced
    return (new_column, diag_block)


def solution(mesh):
    in_specs = (P("prow", "pcol"), P(None, "prow", "pcol"), P(), P(), P())
    out_specs = (P(None, "prow", "pcol"), P(None, "prow", "pcol"))
    return jax.shard_map(local, mesh=mesh, in_specs=in_specs, out_specs=out_specs, check_vma=False)
```

profile of v0, /device:TPU:0, one launch (start us, length us, event | category | flops | bytes accessed | tf_op | source)
XLA Modules:
  0.0 451.2 jit_solution(8875050085147239257)
XLA Ops:
  7.2 0.0 all-gather.2.cloned.1.call-start
  7.2 0.9 iota_compare_fusion
  8.1 0.9 and_reduce_fusion
  9.0 0.1 broadcast_in_dim.2
  9.1 0.1 mul.33
  9.1 9.9 %all_gather.6 = f32[2,128,512]{2,1,0:T(8,128)S(1)} all-gather(f32[2,128,128]{2,1,0:T(8,128)} %param.6), channel_id=1, replica_groups=mesh['prow'=32,'pcol'=4] {'pcol'}, dimensions={2}, use_global_device_ids=true | all-gather | bytes 655360 | tf_op jit(solution)/shard_map/all_gather | solution.py:25
  19.0 1.3 convolution_multiply_fusion
  20.3 0.7 constant_dynamic-slice_fusion
  21.0 0.0 reduce-scatter.3.cloned.1.call-start
  21.1 157.6 %all-gather.2.cloned.1.call-done = f32[2,4096,128]{2,1,0:T(8,128)} async-done(((f32[2,128,128]{2,1,0:T(8,128)}), f32[2,4096,128]{2,1,0:T(8,128)}) %all-gather.2.cloned.1.call-update) | async-done | bytes 4194320 | tf_op jit(solution)/shard_map/all_gather | solution.py:30
  178.7 2.5 copy.21
  181.1 53.7 %all_to_all.15 = f32[2,8,4,128,128]{4,3,1,0,2:T(8,128)} all-to-all(f32[2,8,4,128,128]{4,3,1,0,2:T(8,128)S(1)} %copy.21), channel_id=1, replica_groups=mesh['prow'=32,'pcol'=4] {'pcol'}, dimensions={2} | all-to-all | bytes 8388608 | tf_op jit(solution)/shard_map/all_to_all | solution.py:34
  234.9 5.2 %copy.22 = f32[2,8,1,128,4,128]{3,1,5,4,0,2:T(8,128)} copy(f32[2,8,1,128,4,128]{5,3,1,0,4,2:T(8,128)} %bitcast.31) | data formatting | bytes 8388608 | tf_op jit(solution)/shard_map/all_to_all | solution.py:34
  240.1 5.0 %reshape.46 = f32[2,1024,512]{1,2,0:T(8,128)} reshape(f32[2,8,1,128,4,128]{3,1,5,4,0,2:T(8,128)} %copy.22) | data formatting | bytes 8388608 | tf_op jit(solution)/shard_map/reshape | solution.py:35
  245.1 6.4 %convolution_bitcast_fusion = f32[2,128,512]{1,2,0:T(8,128)} fusion(f32[2,1024,512]{1,2,0:T(8,128)} %reshape.46, f32[128,1024]{1,0:T(8,128)S(1)} %copy-done.1), kind=kOutput, calls=%fused_computation | convolution fusion | flops 1610612736 | bytes 5242880 | tf_op jit(solution)/shard_map/rc,scw->srw/dot_general | solution.py:36
  251.5 0.0 reduce-scatter.3.cloned.1.call-update
  251.5 0.0 reduce-scatter.5.cloned.1.call-start
  251.6 27.0 %reduce-scatter.3.cloned.1.call-done = f32[2,128,128]{1,2,0:T(8,128)} async-done(((f32[2,128,512]{1,2,0:T(8,128)}), f32[2,128,128]{1,2,0:T(8,128)}) %reduce-scatter.3.cloned.1.call-update) | async-done | bytes 131088 | tf_op jit(solution)/shard_map/reduce_scatter | solution.py:37
  278.5 1.5 fusion.3
  280.0 1.0 copy.24
  281.0 0.9 multiply_negate_fusion
  282.0 0.8 copy.26
  282.7 159.5 %reduce-scatter.5.cloned.1.call-done = f32[16,256]{1,0:T(8,128)} async-done(((f32[512,256]{1,0:T(8,128)}), f32[16,256]{1,0:T(8,128)}) %reduce-scatter.5.cloned.1.call-update) | async-done | bytes 16400 | tf_op jit(solution)/shard_map/reduce_scatter | solution.py:42
  442.2 2.5 convolution_add_fusion
  (8 shorter events, 0.1 us)
Async XLA Ops:
  7.2 11.8 %copy-start = (f32[2,512,512]{2,1,0:T(8,128)S(1)}, f32[2,512,512]{2,1,0:T(8,128)}, u32[]{:S(2)}) copy-start(f32[2,512,512]{2,1,0:T(8,128)} %param.7) | copy-start | bytes 6291460
  7.2 171.5 %all-gather.2.cloned.1.call-start = ((), (), s32[]{:S(2)}) async-start(), calls=%async_computation.3 | async-start | bytes 4325376 | tf_op jit(solution)/shard_map/all_gather | solution.py:30
  21.0 257.5 %reduce-scatter.3.cloned.1.call-start = ((), (), s32[]{:S(2)}) async-start(), calls=%async_computation.4 | async-start | bytes 655360 | tf_op jit(solution)/shard_map/reduce_scatter | solution.py:37
  240.1 5.0 %copy-start.1 = (f32[128,1024]{1,0:T(8,128)S(1)}, f32[128,1024]{1,0:T(8,128)}, u32[]{:S(2)}) copy-start(f32[128,1024]{1,0:T(8,128)} %param.5) | copy-start | bytes 1572868
  251.5 190.7 %reduce-scatter.5.cloned.1.call-start = ((), (), s32[]{:S(2)}) async-start(), calls=%async_computation.5 | async-start | bytes 540672 | tf_op jit(solution)/shard_map/reduce_scatter | solution.py:42
Sparse Core Ops, SparseCore 0:
  21.1 157.5 all-gather.1
  251.6 26.8 reduce-scatter.2
  281.2 161.0 reduce-scatter.4
where the time goes:
time: 452 us; the launch traced here: 451 us
  waiting for transfers between devices  344 us (76%)
  blocking collectives  63.6 us (14%)
  local copies, waits for them, and re-layouts  15.3 us (3%)
  between operations  13.8 us (3%)
  matrix products  11.7 us (3%)
    reduce_scatter x1, waiting for transfers between devices, local(): lax.psum_scatter(product.reshape(lax.axis_size('prow') * diag_rows, -1),...  159 us
    all_gather x1, waiting for transfers between devices, local(): collected = lax.all_gather(own_part, 'prow', axis=1, tiled=True)  158 us
    all_to_all x1, blocking collectives, local(): lax.all_to_all(grouped, 'pcol', split_axis=2, concat_axis=4, tiled=True)  53.7 us
    reduce_scatter x1, waiting for transfers between devices, local(): lax.psum_scatter(partial_sums, 'pcol', scatter_dimension=2, tiled=True)  27 us
    all_gather x1, blocking collectives, local(): full_panel = lax.all_gather(factor_panel, 'pcol', axis=2, tiled=True)  9.87 us
  transfers between devices with their start and end apart: 3, of which 3 were waited for; matrix products, arithmetic and copies ran while one was open for 0% of the time, Pallas kernels for 0%

commit v1 on v0

--- a/solution.py
+++ b/solution.py
@@ -27,7 +27,7 @@
         jnp.einsum("srk,skw->srw", full_panel, diag_inverse, precision=precise) * row_mask
     )
     own_part = lax.dynamic_slice_in_dim(scaled_panel, col_index * quarter, quarter, 2)
-    collected = lax.all_gather(own_part, "prow", axis=1, tiled=True)
+    collected = jnp.concatenate(jax.lax.all_gather(own_part, axis_name="prow"), axis=1)
     grouped = collected.reshape(
         supernodes, row_devices // col_devices, col_devices, band_rows, quarter
     )

time: 452 us -> 452 us (level)
    another operation x0 -> x1, local copies, waits for them, and re-layouts: none -> 5.25 us  [local(): collected.reshape(supernodes, row_devices // col_devices, col_devices, ba...]
where the time goes in v1:
time: 452 us; the launch traced here: 451 us
  waiting for transfers between devices  344 us (76%)
  blocking collectives  63.7 us (14%)
  local copies, waits for them, and re-layouts  15 us (3%)
  between operations  13.8 us (3%)
  matrix products  11.6 us (3%)
    reduce_scatter x1, waiting for transfers between devices, local(): lax.psum_scatter(product.reshape(lax.axis_size('prow') * diag_rows, -1),...  159 us
    all_gather x1, waiting for transfers between devices, local(): jax.lax.all_gather(own_part, axis_name='prow')  158 us
    all_to_all x1, blocking collectives, local(): lax.all_to_all(grouped, 'pcol', split_axis=2, concat_axis=4, tiled=True)  53.8 us
    reduce_scatter x1, waiting for transfers between devices, local(): lax.psum_scatter(partial_sums, 'pcol', scatter_dimension=2, tiled=True)  27.1 us
    all_gather x1, blocking collectives, local(): full_panel = lax.all_gather(factor_panel, 'pcol', axis=2, tiled=True)  9.87 us
  transfers between devices with their start and end apart: 3, of which 3 were waited for; matrix products, arithmetic and copies ran while one was open for 0% of the time, Pallas kernels for 0%

profile of v1, /device:TPU:0, one launch (start us, length us, event | category | flops | bytes accessed | tf_op | source)
XLA Modules:
  0.0 451.2 jit_solution(14815678304134145412)
XLA Ops:
  7.2 0.0 all-gather.3.cloned.1.call-start
  7.2 0.9 iota_compare_fusion
  8.1 0.9 and_reduce_fusion
  9.0 0.1 broadcast_in_dim.2
  9.1 0.1 mul.33
  9.1 9.9 %all_gather.9 = f32[2,128,512]{2,1,0:T(8,128)S(1)} all-gather(f32[2,128,128]{2,1,0:T(8,128)} %param.6), channel_id=1, replica_groups=mesh['prow'=32,'pcol'=4] {'pcol'}, dimensions={2}, use_global_device_ids=true | all-gather | bytes 655360 | tf_op jit(solution)/shard_map/all_gather | solution.py:25
  19.0 1.3 convolution_multiply_fusion
  20.3 0.7 constant_dynamic-slice_fusion
  21.0 0.0 reduce-scatter.3.cloned.1.call-start
  21.1 157.5 %all-gather.3.cloned.1.call-done = f32[64,128,128]{2,1,0:T(8,128)} async-done(((f32[2,128,128]{2,1,0:T(8,128)}), f32[64,128,128]{2,1,0:T(8,128)}) %all-gather.3.cloned.1.call-update) | async-done | bytes 4194320 | tf_op jit(solution)/shard_map/all_gather | solution.py:30
  178.6 5.2 %copy.34 = f32[2,8,4,128,128]{3,1,4,0,2:T(8,128)} copy(f32[2,8,4,128,128]{4,3,0,2,1:T(8,128)} %bitcast.36) | data formatting | bytes 8388608 | tf_op jit(solution)/shard_map/reshape;reshape | solution.py:31
  183.8 53.8 %all_to_all.15 = f32[2,8,4,128,128]{3,1,4,0,2:T(8,128)S(1)} all-to-all(f32[2,8,4,128,128]{3,1,4,0,2:T(8,128)} %copy.34), channel_id=1, replica_groups=mesh['prow'=32,'pcol'=4] {'pcol'}, dimensions={2} | all-to-all | bytes 8388608 | tf_op jit(solution)/shard_map/all_to_all | solution.py:34
  237.7 2.3 copy.35
  239.9 4.9 %reshape.46 = f32[2,1024,512]{1,2,0:T(8,128)} reshape(f32[2,8,1,128,4,128]{3,1,5,4,0,2:T(8,128)} %copy.35) | data formatting | bytes 8388608 | tf_op jit(solution)/shard_map/reshape | solution.py:35
  244.9 6.4 %convolution_bitcast_fusion = f32[2,128,512]{1,2,0:T(8,128)} fusion(f32[2,1024,512]{1,2,0:T(8,128)} %reshape.46, f32[128,1024]{1,0:T(8,128)S(1)} %copy-done.1), kind=kOutput, calls=%fused_computation | convolution fusion | flops 1610612736 | bytes 5242880 | tf_op jit(solution)/shard_map/rc,scw->srw/dot_general | solution.py:36
  251.3 0.0 reduce-scatter.3.cloned.1.call-update
  251.3 0.0 reduce-scatter.5.cloned.1.call-start
  251.3 27.1 %reduce-scatter.3.cloned.1.call-done = f32[2,128,128]{1,2,0:T(8,128)} async-done(((f32[2,128,512]{1,2,0:T(8,128)}), f32[2,128,128]{1,2,0:T(8,128)}) %reduce-scatter.3.cloned.1.call-update) | async-done | bytes 131088 | tf_op jit(solution)/shard_map/reduce_scatter | solution.py:37
  278.5 1.5 fusion.3
  280.0 1.0 copy.37
  281.0 0.9 multiply_negate_fusion
  281.9 0.8 copy.39
  282.7 159.5 %reduce-scatter.5.cloned.1.call-done = f32[16,256]{1,0:T(8,128)} async-done(((f32[512,256]{1,0:T(8,128)}), f32[16,256]{1,0:T(8,128)}) %reduce-scatter.5.cloned.1.call-update) | async-done | bytes 16400 | tf_op jit(solution)/shard_map/reduce_scatter | solution.py:42
  442.1 2.5 convolution_add_fusion
  (8 shorter events, 0.1 us)
Async XLA Ops:
  7.2 11.8 %copy-start = (f32[2,512,512]{2,1,0:T(8,128)S(1)}, f32[2,512,512]{2,1,0:T(8,128)}, u32[]{:S(2)}) copy-start(f32[2,512,512]{2,1,0:T(8,128)} %param.7) | copy-start | bytes 6291460
  7.2 171.4 %all-gather.3.cloned.1.call-start = ((), (), s32[]{:S(2)}) async-start(), calls=%async_computation.5 | async-start | bytes 4325376 | tf_op jit(solution)/shard_map/all_gather | solution.py:30
  21.0 257.5 %reduce-scatter.3.cloned.1.call-start = ((), (), s32[]{:S(2)}) async-start(), calls=%async_computation.3 | async-start | bytes 655360 | tf_op jit(solution)/shard_map/reduce_scatter | solution.py:37
  239.9 4.9 %copy-start.1 = (f32[128,1024]{1,0:T(8,128)S(1)}, f32[128,1024]{1,0:T(8,128)}, u32[]{:S(2)}) copy-start(f32[128,1024]{1,0:T(8,128)} %param.5) | copy-start | bytes 1572868
  251.3 190.9 %reduce-scatter.5.cloned.1.call-start = ((), (), s32[]{:S(2)}) async-start(), calls=%async_computation.4 | async-start | bytes 540672 | tf_op jit(solution)/shard_map/reduce_scatter | solution.py:42
Sparse Core Ops, SparseCore 0:
  21.1 157.4 all-gather.2
  251.4 27.0 reduce-scatter.2
  281.1 161.0 reduce-scatter.4
